TPU v7x, 256 devices: a whole 4x4x8 slice. The times are simulated.
256 devices in a mesh: row: 16 (over y_lo, z), vec: 16 (over y_hi, x, core).
Axes of the slice: x: 4, y: 4 (y_hi: 2, y_lo: 2; y = y_hi * 2 + y_lo), z: 8, core: 2. Of those that a mesh axis runs over, the one named last changes fastest.
Arguments:
- vectors: float32 [16384, 6144], P('row', 'vec'), may hold values from -6 to 6
- reflectors: float32 [64, 512, 256], P('row', 'vec'), may hold values from -0.25 to 0.25
- inner_factors: float32 [64, 256, 256], P('row', 'vec'), may hold values from -0.375 to 0.375
- offsets: int32 [2, 32], P(None, 'row'), may hold values from 0 to 15872, as said below
- owners: int32 [2, 32], P(None, 'row'), may hold values from 0 to 3, as said below
Outputs:
- result: float32 [16384, 6144], P('row', 'vec')
Inputs may be any that keep to these rules, and one draw needn't show every extreme that they name: `offsets`: within each sweep the columns j * 2 to (j + 1) * 2 - 1 belong to panel j, the rows j * 1024 to (j + 1) * 1024 - 1; a panel's start rows increase and are multiples of 256. A first-sweep block lies within its panel. A second-sweep block starts 256 rows or more after its panel's first row; in every panel but the last, the last second-sweep block starts at the panel's end minus 256, so it runs 256 rows into the next panel; the last panel's second-sweep blocks lie within it. `owners`: for each panel, its 4 entries (both sweeps) are a permutation of 0 to 3.
All inputs are finite; a program needn't handle non-finite values.
Results may differ from a plain program's by a relative error of at most 0.0001.
Values sent between devices are 32-bit elements; how exact they have to be, the bound alone decides.
No kernel may reach another device: no remote copies, remote signals or barrier semaphores. Data moves between devices by JAX's collectives and lax.ppermute only.
A program may use at most 64 MiB of HBM per device.

v0:
```python
import jax
import jax.numpy as jnp
from jax import lax
from jax.sharding import PartitionSpec as P


def from_behind(block, axis, distance):
    devices = range(lax.axis_size(axis))
    route = [(i - distance, i) for i in devices if i - distance in devices]
    return lax.ppermute(block, axis, route)


def contract_rows(left, right):
    return lax.dot_general(
        left,
        right,
        (((0,), (0,)), ((), ())),
        precision=lax.Precision.HIGHEST,
        preferred_element_type=jnp.float32,
    )


def multiply(left, right):
    return jnp.dot(left, right, precision=lax.Precision.HIGHEST, preferred_element_type=jnp.float32)


def shards(vectors, reflectors, inner_factors, offsets, owners):
    rows_dev = vectors.shape[0]
    reflect_count = reflectors.shape[2]
    block_rows = 2 * reflect_count
    per_sweep = offsets.shape[1]
    first_row = lax.axis_index("row") * rows_dev

    def fetch_block(owner_code):
        stored_basis = lax.dynamic_index_in_dim(reflectors, owner_code, 0, keepdims=False)
        stored_inner = lax.dynamic_index_in_dim(inner_factors, owner_code, 0, keepdims=False)
        return (
            lax.all_gather(stored_basis, "vec", axis=0, tiled=True),
            lax.all_gather(stored_inner, "vec", axis=0, tiled=True),
        )

    def run_sweep(current, sweep_index):

        def apply_block(block_index, current_rows):
            start_row = offsets[sweep_index, block_index] - first_row
            basis_block, inner_block = fetch_block(owners[sweep_index, block_index])
            window = lax.dynamic_slice_in_dim(current_rows, start_row, block_rows, 0)
            projection = contract_rows(basis_block, window)
            coupled = multiply(inner_block, projection)
            window = window - multiply(basis_block, coupled)
            return lax.dynamic_update_slice_in_dim(current_rows, window, start_row, 0)

        return lax.fori_loop(0, per_sweep, apply_block, current)

    after_first = run_sweep(vectors, 0)
    below_rows = from_behind(after_first[:reflect_count], "row", -1)
    extended = jnp.concatenate([after_first, below_rows], 0)
    extended = run_sweep(extended, 1)
    handed = from_behind(extended[rows_dev:], "row", 1)
    head_rows = jnp.where(lax.axis_index("row") > 0, handed, extended[:reflect_count])
    return jnp.concatenate([head_rows, extended[reflect_count:rows_dev]], 0)


def solution(mesh):
    return jax.shard_map(
        shards,
        mesh=mesh,
        in_specs=(
            P("row", "vec"),
            P("row", "vec", None),
            P("row", "vec", None),
            P(None, "row"),
            P(None, "row"),
        ),
        out_specs=P("row", "vec"),
        check_vma=False,
    )
```

profile of v0, /device:TPU:10, one launch (start us, length us, event | category | flops | bytes accessed | tf_op | source)
XLA Modules:
  0.0 253.6 jit_solution(5335601532820274075)
XLA Ops:
  0.0 1.4 copy-done
  1.4 109.5 %while.26 = (s32[]{:T(128)}, f32[1024,384]{1,0:T(8,128)S(1)}, s32[2,2]{1,0:T(2,128)S(1)}, s32[]{:T(128)}, s32[2,2]{1,0:T(2,128)S(1)}, /*index=5*/f32[4,32,256]{2...) while((s32[]{:T(128)}, f32[1024,384]{1,0:T(8,128)S(1)}, ...), condition=%wide.region_1.2_spmd, body=%wide.region_0.1_spmd.sunk | while | flops 1510146048 | bytes 7749873 | solution.py:53
  7.0 20.2 %all-gather.9 = f32[1,256,256]{2,1,0:T(8,128)S(1)} all-gather(f32[1,16,256]{2,1,0:T(8,128)S(1)} %constant_dynamic-slice_fusion.19), channel_id=3, replica_groups=mesh['row'=16,'vec'=16] {'vec'}, dimensions={1}, use_global_device_ids=true | all-gather | bytes 278528 | tf_op jit(solution)/shard_map/while/body/eval_jaxpr/all_gather | solution.py:39
  27.2 24.8 %all-gather.8 = f32[1,512,256]{2,1,0:T(8,128)S(1)} all-gather(f32[1,32,256]{2,1,0:T(8,128)S(1)} %constant_dynamic-slice_fusion.18), channel_id=2, replica_groups=mesh['row'=16,'vec'=16] {'vec'}, dimensions={1}, use_global_device_ids=true | all-gather | bytes 557056 | tf_op jit(solution)/shard_map/while/body/eval_jaxpr/all_gather | solution.py:38
  52.0 1.1 fusion.40
  54.7 3.0 %dynamic_update_slice.16 = f32[1024,384]{1,0:T(8,128)S(1)} dynamic-update-slice(f32[1024,384]{1,0:T(8,128)S(1)} %get-tuple-element.381, f32[512,384]{1,0:T(8,128)S(1)} %convolution_subtract_fusion.4, s32[]{:T(128)S(6)} %select_n.62, s32[]{:T(128)} %constant.85.clone.1..sunk) | dynamic-update-slice | bytes 1572868 | tf_op jit(solution)/shard_map/while/body/eval_jaxpr/dynamic_update_slice | solution.py:51
  63.3 20.0 %all-gather.9 = f32[1,256,256]{2,1,0:T(8,128)S(1)} all-gather(f32[1,16,256]{2,1,0:T(8,128)S(1)} %constant_dynamic-slice_fusion.19), channel_id=3, replica_groups=mesh['row'=16,'vec'=16] {'vec'}, dimensions={1}, use_global_device_ids=true | all-gather | bytes 278528 | tf_op jit(solution)/shard_map/while/body/eval_jaxpr/all_gather | solution.py:39
  83.3 22.0 %all-gather.8 = f32[1,512,256]{2,1,0:T(8,128)S(1)} all-gather(f32[1,32,256]{2,1,0:T(8,128)S(1)} %constant_dynamic-slice_fusion.18), channel_id=2, replica_groups=mesh['row'=16,'vec'=16] {'vec'}, dimensions={1}, use_global_device_ids=true | all-gather | bytes 557056 | tf_op jit(solution)/shard_map/while/body/eval_jaxpr/all_gather | solution.py:38
  105.3 1.1 fusion.40
  108.0 2.9 %dynamic_update_slice.16 = f32[1024,384]{1,0:T(8,128)S(1)} dynamic-update-slice(f32[1024,384]{1,0:T(8,128)S(1)} %get-tuple-element.381, f32[512,384]{1,0:T(8,128)S(1)} %convolution_subtract_fusion.4, s32[]{:T(128)S(6)} %select_n.62, s32[]{:T(128)} %constant.85.clone.1..sunk) | dynamic-update-slice | bytes 1572868 | tf_op jit(solution)/shard_map/while/body/eval_jaxpr/dynamic_update_slice | solution.py:51
  110.9 8.5 %collective-permute-start = (f32[256,384]{1,0:T(8,128)S(1)}, f32[256,384]{1,0:T(8,128)}, u32[]{:S(2)}, u32[]{:S(2)}) collective-permute-start(f32[256,384]{1,0:T(8,128)S(1)} %slice.12), channel_id=1, source_target_pairs={{16,0},{32,16},{48,32},{64,48},{80,64},{96,80},{112,96},{128,112},... | collective-permute-start | bytes 1179656 | tf_op jit(solution)/shard_map/ppermute | solution.py:10
  119.5 8.9 %collective-permute-done = f32[256,384]{1,0:T(8,128)} collective-permute-done((f32[256,384]{1,0:T(8,128)S(1)}, f32[256,384]{1,0:T(8,128)}, u32[]{:S(2)}, u32[]{:S(2)}) %collective-permute-start) | collective-permute-done | bytes 393248 | tf_op jit(solution)/shard_map/ppermute | solution.py:10
  128.4 1.1 pad_maximum_fusion
  129.5 106.5 %while.27 = (s32[]{:T(128)}, f32[1280,384]{1,0:T(8,128)S(1)}, s32[2,2]{1,0:T(2,128)S(1)}, s32[]{:T(128)}, s32[2,2]{1,0:T(2,128)S(1)}, /*index=5*/f32[4,32,256]{2...) while((s32[]{:T(128)}, f32[1280,384]{1,0:T(8,128)S(1)}, ...), condition=%wide.region_3.4_spmd, body=%wide.region_2.3_spmd.sunk | while | flops 1510146048 | bytes 7749873 | solution.py:53
  135.1 20.0 %all-gather.11 = f32[1,256,256]{2,1,0:T(8,128)S(1)} all-gather(f32[1,16,256]{2,1,0:T(8,128)S(1)} %constant_dynamic-slice_fusion.23), channel_id=5, replica_groups=mesh['row'=16,'vec'=16] {'vec'}, dimensions={1}, use_global_device_ids=true | all-gather | bytes 278528 | tf_op jit(solution)/shard_map/while/body/eval_jaxpr/all_gather | solution.py:39
  155.1 22.0 %all-gather.10 = f32[1,512,256]{2,1,0:T(8,128)S(1)} all-gather(f32[1,32,256]{2,1,0:T(8,128)S(1)} %constant_dynamic-slice_fusion.22), channel_id=4, replica_groups=mesh['row'=16,'vec'=16] {'vec'}, dimensions={1}, use_global_device_ids=true | all-gather | bytes 557056 | tf_op jit(solution)/shard_map/while/body/eval_jaxpr/all_gather | solution.py:38
  179.8 3.0 %dynamic_update_slice.17 = f32[1280,384]{1,0:T(8,128)S(1)} dynamic-update-slice(f32[1280,384]{1,0:T(8,128)S(1)} %get-tuple-element.414, f32[512,384]{1,0:T(8,128)S(1)} %convolution_subtract_fusion.5, s32[]{:T(128)S(6)} %select_n.64, s32[]{:T(128)} %constant.85.clone.1..sunk.1) | dynamic-update-slice | bytes 1572868 | tf_op jit(solution)/shard_map/while/body/eval_jaxpr/dynamic_update_slice | solution.py:51
  188.4 20.0 %all-gather.11 = f32[1,256,256]{2,1,0:T(8,128)S(1)} all-gather(f32[1,16,256]{2,1,0:T(8,128)S(1)} %constant_dynamic-slice_fusion.23), channel_id=5, replica_groups=mesh['row'=16,'vec'=16] {'vec'}, dimensions={1}, use_global_device_ids=true | all-gather | bytes 278528 | tf_op jit(solution)/shard_map/while/body/eval_jaxpr/all_gather | solution.py:39
  208.3 22.0 %all-gather.10 = f32[1,512,256]{2,1,0:T(8,128)S(1)} all-gather(f32[1,32,256]{2,1,0:T(8,128)S(1)} %constant_dynamic-slice_fusion.22), channel_id=4, replica_groups=mesh['row'=16,'vec'=16] {'vec'}, dimensions={1}, use_global_device_ids=true | all-gather | bytes 557056 | tf_op jit(solution)/shard_map/while/body/eval_jaxpr/all_gather | solution.py:38
  230.4 1.1 fusion.48
  233.0 2.9 %dynamic_update_slice.17 = f32[1280,384]{1,0:T(8,128)S(1)} dynamic-update-slice(f32[1280,384]{1,0:T(8,128)S(1)} %get-tuple-element.414, f32[512,384]{1,0:T(8,128)S(1)} %convolution_subtract_fusion.5, s32[]{:T(128)S(6)} %select_n.64, s32[]{:T(128)} %constant.85.clone.1..sunk.1) | dynamic-update-slice | bytes 1572868 | tf_op jit(solution)/shard_map/while/body/eval_jaxpr/dynamic_update_slice | solution.py:51
  236.0 1.9 collective-permute-start.1
  238.1 14.2 %collective-permute-done.1 = f32[256,384]{1,0:T(8,128)S(1)} collective-permute-done((f32[256,384]{1,0:T(8,128)S(1)}, f32[256,384]{1,0:T(8,128)S(1)}, u32[]{:S(2)}, u32[]{:S(2)}) %collective-permute-start.1) | collective-permute-done | bytes 393248 | tf_op jit(solution)/shard_map/ppermute | solution.py:10
  252.3 1.2 pad_maximum_fusion.1
  (34 shorter events, 18.9 us)
Async XLA Ops:
  0.0 1.4 copy-start
  0.0 1.4 copy-start.1
  0.0 1.4 copy-start.2
  110.9 17.4 %collective-permute-start = (f32[256,384]{1,0:T(8,128)S(1)}, f32[256,384]{1,0:T(8,128)}, u32[]{:S(2)}, u32[]{:S(2)}) collective-permute-start(f32[256,384]{1,0:T(8,128)S(1)} %slice.12), channel_id=1, source_target_pairs={{16,0},{32,16},{48,32},{64,48},{80,64},{96,80},{112,96},{128,112},... | collective-permute-start | bytes 1179656 | tf_op jit(solution)/shard_map/ppermute | solution.py:10
  236.0 16.2 %collective-permute-start.1 = (f32[256,384]{1,0:T(8,128)S(1)}, f32[256,384]{1,0:T(8,128)S(1)}, u32[]{:S(2)}, u32[]{:S(2)}) collective-permute-start(f32[256,384]{1,0:T(8,128)S(1)} %slice.13), channel_id=1, source_target_pairs={{0,16},{16,32},{32,48},{48,64},{64,80},{80,96},{96,112},{112,128},... | collective-permute-start | bytes 1179656 | tf_op jit(solution)/shard_map/ppermute | solution.py:10
where the time goes:
time: 254 us
  blocking collectives  171 us (67%)
  local copies, waits for them, and re-layouts  24.7 us (10%)
  waiting for transfers between devices  23.1 us (9%)
  loops' own time  11.3 us (4%)
  matrix products  10.6 us (4%)
  starting transfers between devices  10.5 us (4%)
    all_gather x4, blocking collectives, fetch_block(): lax.all_gather(stored_basis, 'vec', axis=0, tiled=True)  90.9 us
    all_gather x4, blocking collectives, fetch_block(): lax.all_gather(stored_inner, 'vec', axis=0, tiled=True)  80 us
    ppermute x2, waiting for transfers between devices, from_behind(): return lax.ppermute(block, axis, route)  23.1 us
    dynamic_update_slice x4, local copies, waits for them, and re-layouts, apply_block(): return lax.dynamic_update_slice_in_dim(current_rows, window, start_row, 0)  11.9 us
    another operation x2, loops' own time, run_sweep(): return lax.fori_loop(0, per_sweep, apply_block, current)  11.3 us
    ppermute x2, starting transfers between devices, from_behind(): return lax.ppermute(block, axis, route)  10.5 us
    dot_general x8, matrix products, multiply(): jnp.dot(left, right, precision=lax.Precision.HIGHEST, preferred_element_t...  6.36 us
  transfers between devices with their start and end apart: 2, of which 2 were waited for; matrix products, arithmetic and copies ran while one was open for 0% of the time, Pallas kernels for 0%

commit v1 on v0

--- a/solution.py
+++ b/solution.py
@@ -35,7 +35,10 @@
         stored_basis = lax.dynamic_index_in_dim(reflectors, owner_code, 0, keepdims=False)
         stored_inner = lax.dynamic_index_in_dim(inner_factors, owner_code, 0, keepdims=False)
         return (
-            lax.all_gather(stored_basis, "vec", axis=0, tiled=True),
+            jnp.concatenate(
+                lax.all_to_all(jnp.stack([stored_basis] * lax.axis_size("vec")), "vec", 0, 0),
+                axis=0,
+            ),
             lax.all_gather(stored_inner, "vec", axis=0, tiled=True),
         )
 

time: 254 us -> 202 us (0.80)
  blocking collectives: 171 us -> 92.7 us
  starting transfers between devices: 10.5 us -> 33.6 us
    all_gather x4 -> x0, blocking collectives: 90.9 us -> none  [fetch_block(): lax.all_gather(stored_basis, 'vec', axis=0, tiled=True)]
    all_to_all x0 -> x4, starting transfers between devices: none -> 23.2 us  [fetch_block(): lax.all_to_all(jnp.stack([stored_basis] * lax.axis_size('vec')), 'vec', 0...]
    all_gather x4, blocking collectives: 80 us -> 92.7 us  [fetch_block(): lax.all_gather(stored_inner, 'vec', axis=0, tiled=True)]
    another operation x0 -> x4, local copies, waits for them, and re-layouts: none -> 3.38 us  [fetch_block(): jnp.stack([stored_basis] * lax.axis_size('vec'))]
    dynamic_slice x4, local copies, waits for them, and re-layouts: 3.04 us -> 0.04 us  [fetch_block(): lax.dynamic_index_in_dim(reflectors, owner_code, 0, keepdims=False)]
    dynamic_slice x4, local copies, waits for them, and re-layouts: 2.89 us -> 0.04 us  [fetch_block(): lax.dynamic_index_in_dim(inner_factors, owner_code, 0, keepdims=False)]
    while x0 -> x8, local copies, waits for them, and re-layouts: none -> 2.62 us
  transfers between devices with their start and end apart: 2 -> 6, of which waited for: 2 -> 2; matrix products, arithmetic and copies ran while one was open for 0% -> 2% of each run, Pallas kernels for 0% -> 0%
where the time goes in v1:
time: 202 us; the launch traced here: 200 us
  blocking collectives  92.7 us (46%)
  starting transfers between devices  33.6 us (17%)
  local copies, waits for them, and re-layouts  26.7 us (13%)
  waiting for transfers between devices  21.7 us (11%)
  loops' own time  10.6 us (5%)
  matrix products  10.6 us (5%)
  other arithmetic  3.73 us (2%)
    all_gather x4, blocking collectives, fetch_block(): lax.all_gather(stored_inner, 'vec', axis=0, tiled=True)  92.7 us
    all_to_all x4, starting transfers between devices, fetch_block(): lax.all_to_all(jnp.stack([stored_basis] * lax.axis_size('vec')), 'vec', 0...  23.2 us
    ppermute x2, waiting for transfers between devices, from_behind(): return lax.ppermute(block, axis, route)  21.7 us
    dynamic_update_slice x4, local copies, waits for them, and re-layouts, apply_block(): return lax.dynamic_update_slice_in_dim(current_rows, window, start_row, 0)  11.9 us
    another operation x2, loops' own time, run_sweep(): return lax.fori_loop(0, per_sweep, apply_block, current)  10.6 us
    ppermute x2, starting transfers between devices, from_behind(): return lax.ppermute(block, axis, route)  10.5 us
    dot_general x8, matrix products, multiply(): jnp.dot(left, right, precision=lax.Precision.HIGHEST, preferred_element_t...  6.35 us
    dot_general x4, matrix products, contract_rows(): lax.dot_general(left, right, (((0,), (0,)), ((), ())), precision=lax.Prec...  4.26 us
  transfers between devices with their start and end apart: 6, of which 2 were waited for; matrix products, arithmetic and copies ran while one was open for 2% of the time, Pallas kernels for 0%

profile of v1, /device:TPU:10, one launch (start us, length us, event | category | flops | bytes accessed | tf_op | source)
XLA Modules:
  0.0 199.8 jit_solution(16573110879465513029)
XLA Ops:
  0.0 1.4 copy-done
  1.4 79.2 %while.26 = (s32[]{:T(128)}, f32[1024,384]{1,0:T(8,128)S(1)}, s32[2,2]{1,0:T(2,128)S(1)}, s32[]{:T(128)}, s32[2,2]{1,0:T(2,128)S(1)}, /*index=5*/f32[4,32,256]{2...) while((s32[]{:T(128)}, f32[1024,384]{1,0:T(8,128)S(1)}, ...), condition=%wide.region_1.2_spmd, body=%wide.region_0.1_spmd.sunk | while | flops 1510146048 | bytes 9322769 | solution.py:56
  4.8 6.6 %all-to-all-start = ((f32[16,32,256]{2,1,0:T(8,128)}), f32[16,32,256]{2,1,0:T(8,128)S(1)}, u32[]{:S(2)}, u32[]{:S(2)}) async-start(f32[16,32,256]{2,1,0:T(8,128)} %stack.10), calls=%async_computation | async-start | bytes 1048576 | tf_op jit(solution)/shard_map/while/body/eval_jaxpr/all_to_all | solution.py:39
  12.7 23.1 %all-gather.4 = f32[1,256,256]{2,1,0:T(8,128)S(1)} all-gather(f32[1,16,256]{2,1,0:T(8,128)S(1)} %constant_dynamic-slice_fusion.14), channel_id=2, replica_groups=mesh['row'=16,'vec'=16] {'vec'}, dimensions={1}, use_global_device_ids=true | all-gather | bytes 278528 | tf_op jit(solution)/shard_map/while/body/eval_jaxpr/all_gather | solution.py:42
  38.5 3.0 %dynamic_update_slice.16 = f32[1024,384]{1,0:T(8,128)S(1)} dynamic-update-slice(f32[1024,384]{1,0:T(8,128)S(1)} %get-tuple-element.381, f32[512,384]{1,0:T(8,128)S(1)} %convolution_subtract_fusion.4, s32[]{:T(128)S(6)} %select_n.63, s32[]{:T(128)} %constant.85.clone.1..sunk) | dynamic-update-slice | bytes 1572868 | tf_op jit(solution)/shard_map/while/body/eval_jaxpr/dynamic_update_slice | solution.py:54
  44.9 5.5 %all-to-all-start = ((f32[16,32,256]{2,1,0:T(8,128)}), f32[16,32,256]{2,1,0:T(8,128)S(1)}, u32[]{:S(2)}, u32[]{:S(2)}) async-start(f32[16,32,256]{2,1,0:T(8,128)} %stack.10), calls=%async_computation | async-start | bytes 1048576 | tf_op jit(solution)/shard_map/while/body/eval_jaxpr/all_to_all | solution.py:39
  51.7 23.2 %all-gather.4 = f32[1,256,256]{2,1,0:T(8,128)S(1)} all-gather(f32[1,16,256]{2,1,0:T(8,128)S(1)} %constant_dynamic-slice_fusion.14), channel_id=2, replica_groups=mesh['row'=16,'vec'=16] {'vec'}, dimensions={1}, use_global_device_ids=true | all-gather | bytes 278528 | tf_op jit(solution)/shard_map/while/body/eval_jaxpr/all_gather | solution.py:42
  77.6 2.9 %dynamic_update_slice.16 = f32[1024,384]{1,0:T(8,128)S(1)} dynamic-update-slice(f32[1024,384]{1,0:T(8,128)S(1)} %get-tuple-element.381, f32[512,384]{1,0:T(8,128)S(1)} %convolution_subtract_fusion.4, s32[]{:T(128)S(6)} %select_n.63, s32[]{:T(128)} %constant.85.clone.1..sunk) | dynamic-update-slice | bytes 1572868 | tf_op jit(solution)/shard_map/while/body/eval_jaxpr/dynamic_update_slice | solution.py:54
  80.6 8.6 %collective-permute-start = (f32[256,384]{1,0:T(8,128)S(1)}, f32[256,384]{1,0:T(8,128)S(1)}, u32[]{:S(2)}, u32[]{:S(2)}) collective-permute-start(f32[256,384]{1,0:T(8,128)S(1)} %slice.12), channel_id=1, source_target_pairs={{16,0},{32,16},{48,32},{64,48},{80,64},{96,80},{112,96},{128,112},... | collective-permute-start | bytes 1179656 | tf_op jit(solution)/shard_map/ppermute | solution.py:10
  89.2 8.9 %collective-permute-done = f32[256,384]{1,0:T(8,128)S(1)} collective-permute-done((f32[256,384]{1,0:T(8,128)S(1)}, f32[256,384]{1,0:T(8,128)S(1)}, u32[]{:S(2)}, u32[]{:S(2)}) %collective-permute-start) | collective-permute-done | bytes 393248 | tf_op jit(solution)/shard_map/ppermute | solution.py:10
  98.0 1.4 pad_maximum_fusion
  99.5 80.9 %while.27 = (s32[]{:T(128)}, f32[1280,384]{1,0:T(8,128)}, s32[2,2]{1,0:T(2,128)S(1)}, s32[]{:T(128)}, s32[2,2]{1,0:T(2,128)S(1)}, /*index=5*/f32[4,32,256]{2,1,0...) while((s32[]{:T(128)}, f32[1280,384]{1,0:T(8,128)}, ...), condition=%wide.region_3.4_spmd, body=%wide.region_2.3_spmd.sunk | while | flops 1510146048 | bytes 25051464 | solution.py:56
  102.9 5.5 %all-to-all-start.1 = ((f32[16,32,256]{2,1,0:T(8,128)}), f32[16,32,256]{2,1,0:T(8,128)S(1)}, u32[]{:S(2)}, u32[]{:S(2)}) async-start(f32[16,32,256]{2,1,0:T(8,128)} %stack.11), calls=%async_computation.1 | async-start | bytes 1048576 | tf_op jit(solution)/shard_map/while/body/eval_jaxpr/all_to_all | solution.py:39
  109.7 23.2 %all-gather.5 = f32[1,256,256]{2,1,0:T(8,128)S(1)} all-gather(f32[1,16,256]{2,1,0:T(8,128)S(1)} %constant_dynamic-slice_fusion.17), channel_id=3, replica_groups=mesh['row'=16,'vec'=16] {'vec'}, dimensions={1}, use_global_device_ids=true | all-gather | bytes 278528 | tf_op jit(solution)/shard_map/while/body/eval_jaxpr/all_gather | solution.py:42
  135.6 3.0 %dynamic_update_slice.17 = f32[1280,384]{1,0:T(8,128)S(1)} dynamic-update-slice(f32[1280,384]{1,0:T(8,128)S(1)} %copy-done.1, f32[512,384]{1,0:T(8,128)S(1)} %convolution_subtract_fusion.5, s32[]{:T(128)S(6)} %select_n.65, s32[]{:T(128)} %constant.85.clone.1..sunk.1) | dynamic-update-slice | bytes 1572868 | tf_op jit(solution)/shard_map/while/body/eval_jaxpr/dynamic_update_slice | solution.py:54
  138.6 1.3 copy-done.2
  143.4 5.5 %all-to-all-start.1 = ((f32[16,32,256]{2,1,0:T(8,128)}), f32[16,32,256]{2,1,0:T(8,128)S(1)}, u32[]{:S(2)}, u32[]{:S(2)}) async-start(f32[16,32,256]{2,1,0:T(8,128)} %stack.11), calls=%async_computation.1 | async-start | bytes 1048576 | tf_op jit(solution)/shard_map/while/body/eval_jaxpr/all_to_all | solution.py:39
  150.2 23.2 %all-gather.5 = f32[1,256,256]{2,1,0:T(8,128)S(1)} all-gather(f32[1,16,256]{2,1,0:T(8,128)S(1)} %constant_dynamic-slice_fusion.17), channel_id=3, replica_groups=mesh['row'=16,'vec'=16] {'vec'}, dimensions={1}, use_global_device_ids=true | all-gather | bytes 278528 | tf_op jit(solution)/shard_map/while/body/eval_jaxpr/all_gather | solution.py:42
  176.1 2.9 %dynamic_update_slice.17 = f32[1280,384]{1,0:T(8,128)S(1)} dynamic-update-slice(f32[1280,384]{1,0:T(8,128)S(1)} %copy-done.1, f32[512,384]{1,0:T(8,128)S(1)} %convolution_subtract_fusion.5, s32[]{:T(128)S(6)} %select_n.65, s32[]{:T(128)} %constant.85.clone.1..sunk.1) | dynamic-update-slice | bytes 1572868 | tf_op jit(solution)/shard_map/while/body/eval_jaxpr/dynamic_update_slice | solution.py:54
  179.0 1.3 copy-done.2
  181.4 1.9 collective-permute-start.1
  183.3 1.3 slice.15
  184.6 12.8 %collective-permute-done.1 = f32[256,384]{1,0:T(8,128)S(1)} collective-permute-done((f32[256,384]{1,0:T(8,128)S(1)}, f32[256,384]{1,0:T(8,128)S(1)}, u32[]{:S(2)}, u32[]{:S(2)}) %collective-permute-start.1) | collective-permute-done | bytes 393248 | tf_op jit(solution)/shard_map/ppermute | solution.py:10
  198.5 1.2 pad_maximum_fusion.1
  (54 shorter events, 21.1 us)
Async XLA Ops:
  0.0 1.4 copy-start
  0.0 1.4 copy-start.3
  0.0 1.4 copy-start.4
  0.0 1.4 copy-start.5
  0.0 1.4 copy-start.6
  4.8 31.0 %all-to-all-start = ((f32[16,32,256]{2,1,0:T(8,128)}), f32[16,32,256]{2,1,0:T(8,128)S(1)}, u32[]{:S(2)}, u32[]{:S(2)}) async-start(f32[16,32,256]{2,1,0:T(8,128)} %stack.10), calls=%async_computation | async-start | bytes 1048576 | tf_op jit(solution)/shard_map/while/body/eval_jaxpr/all_to_all | solution.py:39
  44.9 30.0 %all-to-all-start = ((f32[16,32,256]{2,1,0:T(8,128)}), f32[16,32,256]{2,1,0:T(8,128)S(1)}, u32[]{:S(2)}, u32[]{:S(2)}) async-start(f32[16,32,256]{2,1,0:T(8,128)} %stack.10), calls=%async_computation | async-start | bytes 1048576 | tf_op jit(solution)/shard_map/while/body/eval_jaxpr/all_to_all | solution.py:39
  80.6 17.4 %collective-permute-start = (f32[256,384]{1,0:T(8,128)S(1)}, f32[256,384]{1,0:T(8,128)S(1)}, u32[]{:S(2)}, u32[]{:S(2)}) collective-permute-start(f32[256,384]{1,0:T(8,128)S(1)} %slice.12), channel_id=1, source_target_pairs={{16,0},{32,16},{48,32},{64,48},{80,64},{96,80},{112,96},{128,112},... | collective-permute-start | bytes 1179656 | tf_op jit(solution)/shard_map/ppermute | solution.py:10
  99.5 33.4 %copy-start.1 = (f32[1280,384]{1,0:T(8,128)S(1)}, f32[1280,384]{1,0:T(8,128)}, u32[]{:S(2)}) copy-start(f32[1280,384]{1,0:T(8,128)} %get-tuple-element.414) | copy-start | bytes 5898244 | tf_op jit(solution)/shard_map/while
  102.9 30.0 %all-to-all-start.1 = ((f32[16,32,256]{2,1,0:T(8,128)}), f32[16,32,256]{2,1,0:T(8,128)S(1)}, u32[]{:S(2)}, u32[]{:S(2)}) async-start(f32[16,32,256]{2,1,0:T(8,128)} %stack.11), calls=%async_computation.1 | async-start | bytes 1048576 | tf_op jit(solution)/shard_map/while/body/eval_jaxpr/all_to_all | solution.py:39
  138.6 1.3 copy-start.2
  139.9 33.5 %copy-start.1 = (f32[1280,384]{1,0:T(8,128)S(1)}, f32[1280,384]{1,0:T(8,128)}, u32[]{:S(2)}) copy-start(f32[1280,384]{1,0:T(8,128)} %get-tuple-element.414) | copy-start | bytes 5898244 | tf_op jit(solution)/shard_map/while
  143.4 30.0 %all-to-all-start.1 = ((f32[16,32,256]{2,1,0:T(8,128)}), f32[16,32,256]{2,1,0:T(8,128)S(1)}, u32[]{:S(2)}, u32[]{:S(2)}) async-start(f32[16,32,256]{2,1,0:T(8,128)} %stack.11), calls=%async_computation.1 | async-start | bytes 1048576 | tf_op jit(solution)/shard_map/while/body/eval_jaxpr/all_to_all | solution.py:39
  179.0 1.3 copy-start.2
  181.4 16.1 %collective-permute-start.1 = (f32[256,384]{1,0:T(8,128)S(1)}, f32[256,384]{1,0:T(8,128)S(1)}, u32[]{:S(2)}, u32[]{:S(2)}) collective-permute-start(f32[256,384]{1,0:T(8,128)S(1)} %slice.13), channel_id=1, source_target_pairs={{0,16},{16,32},{32,48},{48,64},{64,80},{80,96},{96,112},{112,128},... | collective-permute-start | bytes 1179656 | tf_op jit(solution)/shard_map/ppermute | solution.py:10
